TPU v7x, 512 devices: a whole 4x8x8 slice. The times are simulated.
512 devices in a mesh: lat: 64 (over y_lo, x, z), lon: 8 (over y_hi, core).
Axes of the slice: x: 4, y: 8 (y_hi: 4, y_lo: 2; y = y_hi * 2 + y_lo), z: 8, core: 2. Of those that a mesh axis runs over, the one named last changes fastest.
Arguments:
- coefficients: float32 [256, 2, 3, 2, 513], P('lat'), may hold values from -0.03125 to 0.03125
- pair_orders: int32 [256], replicated, may hold values from 0 to 255, each once
Outputs:
- potential: float32 [3, 2, 1024, 2048], P(None, None, 'lat', 'lon')
- magnetic_field: float32 [3, 2, 1024, 2048], P(None, None, 'lat', 'lon')
Inputs may be any that keep to these rules, and one draw needn't show every extreme that they name: A permutation of 0 to 255; row p of coefficients holds the orders pair_orders[p] and 511 - pair_orders[p].
All inputs are finite; a program needn't handle non-finite values.
Results may differ from a plain program's by a relative error of at most 0.0003.
Values sent between devices are 32-bit elements; how exact they have to be, the bound alone decides.
No kernel may reach another device: no remote copies, remote signals or barrier semaphores. Data moves between devices by JAX's collectives and lax.ppermute only.
A program may use at most 64 MiB of HBM per device.

v0:
```python
import math
import jax
import jax.numpy as jnp
from jax import lax
from jax.sharding import PartitionSpec as P

NT = 1024
NP = 2048
STEPS = 2
soft_floor = 1.0
resist = 0.2
time_step = 0.3
rescale_at = 10000000000.0
block_steps = 128
span_start = math.pi / 6.0
span_width = 2.0 * math.pi / 3.0


def with_halo(value, sides, width, wrap):
    for axis, dim in sides:
        size, length = (lax.axis_size(axis), value.shape[dim])
        up = [(i, (i + 1) % size) for i in range(size if wrap else size - 1)]
        down = [(j, i) for i, j in up]
        last = lax.slice_in_dim(value, length - width, length, axis=dim)
        first = lax.slice_in_dim(value, 0, width, axis=dim)
        before = lax.ppermute(last, axis, up)
        after = lax.ppermute(first, axis, down)
        value = jnp.concatenate([before, value, after], axis=dim)
    return value


def row_angles(row_ids, row_total):
    return span_start + (row_ids.astype(jnp.float32) + 0.5) * (span_width / row_total)


def norm_logs(order_total):
    degrees = jnp.arange(1, order_total, dtype=jnp.float32)
    log_terms = 0.5 * jnp.log((2.0 * degrees + 1.0) / (2.0 * degrees))
    return jnp.concatenate([jnp.zeros((1,), jnp.float32), jnp.cumsum(log_terms)]) - 0.5 * jnp.log(
        4.0 * math.pi
    )


def pick_logs(log_table, orders):
    order_grid = jnp.arange(log_table.shape[0], dtype=jnp.int32)
    return jnp.sum(
        jnp.where(order_grid[None, :] == orders[:, None], log_table[None, :], 0.0), axis=1
    )


def synthesize(coef_rows, small_orders, angles, order_total):
    pair_count = coef_rows.shape[0]
    columns = coef_rows.shape[1] * coef_rows.shape[2] * coef_rows.shape[3]
    packed = coef_rows.shape[4]
    block_count = -(-packed // block_steps)
    padded = block_count * block_steps
    flat_coef = jnp.pad(
        coef_rows.reshape(pair_count, columns, packed), ((0, 0), (0, 0), (0, padded - packed))
    )
    large_orders = order_total - 1 - small_orders
    low_order = small_orders.astype(jnp.float32)
    high_order = large_orders.astype(jnp.float32)
    switch = order_total - low_order
    positions = jnp.arange(padded, dtype=jnp.float32)
    low_mask = (positions[None, :] < switch[:, None]).astype(jnp.float32)
    masked = flat_coef[:, None, :, :] * jnp.stack([low_mask, 1.0 - low_mask], axis=1)[:, :, None, :]
    log_table = norm_logs(order_total)
    log_sin = jnp.log(jnp.sin(angles))
    cosine = jnp.cos(angles)
    seed_low = pick_logs(log_table, small_orders)[:, None] + low_order[:, None] * log_sin[None, :]
    seed_high = pick_logs(log_table, large_orders)[:, None] + high_order[:, None] * log_sin[None, :]
    log_big = math.log(rescale_at)

    def advance(carried, step_now):
        previous, current, scaling = carried
        low_side = step_now < switch
        order_now = jnp.where(low_side, low_order, high_order)
        degree = jnp.where(low_side, low_order + step_now, step_now - 1.0)
        starting = (degree == order_now)[:, None]
        factor = jnp.sqrt(
            jnp.maximum(4.0 * degree * degree - 1.0, 1.0)
            / jnp.maximum(degree * degree - order_now * order_now, 1.0)
        )
        prior_degree = degree - 1.0
        back_factor = jnp.where(
            prior_degree > order_now,
            jnp.sqrt(
                (prior_degree * prior_degree - order_now * order_now)
                / jnp.maximum(4.0 * prior_degree * prior_degree - 1.0, 1.0)
            ),
            0.0,
        )
        next_value = factor[:, None] * (cosine[None, :] * current - back_factor[:, None] * previous)
        seed_now = jnp.where(low_side[:, None], seed_low, seed_high)
        previous = jnp.where(starting, 0.0, current)
        current = jnp.where(starting, 1.0, next_value)
        scaling = jnp.where(starting, seed_now, scaling)
        too_big = jnp.abs(current) > rescale_at
        shrink = jnp.where(too_big, 1.0 / rescale_at, 1.0)
        previous = previous * shrink
        current = current * shrink
        scaling = scaling + jnp.where(too_big, log_big, 0.0)
        return ((previous, current, scaling), current * jnp.exp(scaling))

    def run_block(carried, block_index):
        rec_state, synth_sum = carried
        step_values = block_index.astype(jnp.float32) * block_steps + jnp.arange(
            block_steps, dtype=jnp.float32
        )
        rec_state, values = lax.scan(advance, rec_state, step_values, unroll=8)
        coef_block = lax.dynamic_slice_in_dim(masked, block_index * block_steps, block_steps, 3)
        synth_sum = synth_sum + jnp.einsum(
            "spt,pkcs->pkct",
            values,
            coef_block,
            precision=lax.Precision.HIGHEST,
            preferred_element_type=jnp.float32,
        )
        return ((rec_state, synth_sum), None)

    zero_rows = jnp.zeros((pair_count, angles.shape[0]), jnp.float32)
    zero_sum = jnp.zeros((pair_count, 2, columns, angles.shape[0]), jnp.float32)
    scanned = lax.scan(
        run_block,
        ((zero_rows, zero_rows, zero_rows), zero_sum),
        jnp.arange(block_count, dtype=jnp.int32),
    )
    synth_sum = scanned[0][1]
    return synth_sum.reshape(pair_count * 2, 2, columns // 2, angles.shape[0])


def sector_table(slot_orders, column_start, col_count, point_total):
    column_ids = column_start + jnp.arange(col_count, dtype=jnp.int32)
    turn_count = slot_orders[:, None] * column_ids[None, :] % point_total
    phase_angle = turn_count.astype(jnp.float32) * (2.0 * math.pi / point_total)
    return jnp.stack([jnp.cos(phase_angle), jnp.sin(phase_angle)], axis=1)


def transform(rows_part, sector_basis):
    return jnp.einsum(
        "gxcr,gxf->crf",
        rows_part,
        sector_basis,
        precision=lax.Precision.HIGHEST,
        preferred_element_type=jnp.float32,
    )


def curl(padded, row_sin, phi_ratio):
    center = padded[:, :, 1:-1, 1:-1]
    theta_diff = 0.5 * (padded[:, :, 2:, 1:-1] - padded[:, :, :-2, 1:-1])
    phi_scale = (1.0 / (2.0 * phi_ratio * row_sin))[None, :, None]
    lifted = jnp.pad(center, ((0, 0), (1, 1), (0, 0), (0, 0)))
    radial_diff = 0.5 * (lifted[:, 2:] - lifted[:, :-2])
    phi_radial = (padded[0, :, 1:-1, 2:] - padded[0, :, 1:-1, :-2]) * phi_scale
    phi_theta = (padded[1, :, 1:-1, 2:] - padded[1, :, 1:-1, :-2]) * phi_scale
    return jnp.stack(
        [theta_diff[2] - phi_theta, phi_radial - radial_diff[2], radial_diff[1] - theta_diff[0]]
    )


def cross_product(first_vec, second_vec):
    return jnp.stack(
        [
            first_vec[1] * second_vec[2] - first_vec[2] * second_vec[1],
            first_vec[2] * second_vec[0] - first_vec[0] * second_vec[2],
            first_vec[0] * second_vec[1] - first_vec[1] * second_vec[0],
        ]
    )


def drift(magnetic, current):
    lorentz = cross_product(current, magnetic)
    velocity = lorentz / (jnp.sum(magnetic * magnetic, axis=0) + soft_floor)
    return cross_product(velocity, magnetic) - resist * current


def per_device(coefficients, pair_orders):
    lat_count = lax.axis_size("lat")
    lon_count = lax.axis_size("lon")
    lat_pos = lax.axis_index("lat")
    lon_pos = lax.axis_index("lon")
    pair_local = coefficients.shape[0]
    levels = coefficients.shape[3]
    order_total = 2 * pair_orders.shape[0]
    row_total = NT
    point_total = NP
    band_rows = row_total // lat_count
    sector_cols = point_total // lon_count
    own_pairs = lax.dynamic_slice_in_dim(pair_orders, lat_pos * pair_local, pair_local)
    slot_orders = jnp.stack([pair_orders, order_total - 1 - pair_orders], axis=1).reshape(
        order_total
    )
    own_table = sector_table(slot_orders, lon_pos * sector_cols, sector_cols, point_total)
    angles = row_angles(jnp.arange(row_total, dtype=jnp.int32), row_total)
    spectral = synthesize(coefficients, own_pairs, angles, order_total)
    synth_grid = transform(
        lax.all_to_all(spectral, "lat", split_axis=3, concat_axis=0, tiled=True), own_table
    )
    potential = synth_grid.reshape(3, levels, band_rows, sector_cols)
    global_rows = lat_pos * band_rows + jnp.arange(-2, band_rows + 2, dtype=jnp.int32)
    sin_all = jnp.sin(row_angles(global_rows, row_total))
    sin_inner = sin_all[2:-2]
    phi_ratio = 3.0 * row_total / point_total
    magnetic = potential

    def extend_rims(values):
        taller = with_halo(values, (("lat", 2),), 1, False)
        return with_halo(taller, (("lon", 3),), 1, True)

    for step_now in range(STEPS):
        magnetic = curl(extend_rims(potential), sin_inner, phi_ratio)
        current = curl(extend_rims(magnetic), sin_inner, phi_ratio)
        potential = potential + time_step * drift(magnetic, current)
    return (potential, magnetic)


def solution(mesh):
    in_specs = (P("lat", None, None, None, None), P())
    out_specs = (P(None, None, "lat", "lon"), P(None, None, "lat", "lon"))
    return jax.shard_map(
        per_device, mesh=mesh, in_specs=in_specs, out_specs=out_specs, check_vma=False
    )
```

profile of v0, /device:TPU:8, one launch (start us, length us, event | category | flops | bytes accessed | tf_op | source)
XLA Modules:
  0.0 1125.7 jit_solution(11292824940193635866)
XLA Ops:
  3.7 957.0 %while.59 = (s32[]{:T(128)}, f32[4,1024]{1,0:T(4,128)S(1)}, f32[4,1024]{1,0:T(4,128)S(1)}, f32[4,1024]{1,0:T(4,128)S(1)}, f32[4,2,12,1024]{3,2,1,0:T(8,128)S(1)}...) while((s32[]{:T(128)}, f32[4,1024]{1,0:T(4,128)S(1)}, ...), condition=%wide.region_7.8_spmd.clone.clone.clone.clone, body=%wide.region_4.7_spmd.clone.clone.clone.clone.sunk | while | flops 152044704 | bytes 4487110 | solution.py:123
  5.0 187.1 %while.60 = (s32[]{:T(128)}, f32[4,1024]{1,0:T(4,128)S(1)}, f32[4,1024]{1,0:T(4,128)S(1)}, f32[4,1024]{1,0:T(4,128)S(1)}, f32[16,8,4,1024]{3,2,1,0:T(4,128)S(1)}...) while((s32[]{:T(128)}, f32[4,1024]{1,0:T(4,128)S(1)}, ...), condition=%wide.region_6.6_spmd.clone, body=%wide.region_5.5_spmd.clone.sunk | while | flops 832281 | bytes 1364985 | solution.py:110
  13.2 2.5 fusion.179
  24.8 2.5 fusion.179
  48.2 2.5 fusion.179
  59.9 2.5 fusion.179
  71.6 2.5 fusion.179
  118.4 2.5 fusion.179
  130.1 2.5 fusion.179
  141.8 2.5 fusion.179
  188.6 2.5 fusion.179
  196.4 187.1 %while.60 = (s32[]{:T(128)}, f32[4,1024]{1,0:T(4,128)S(1)}, f32[4,1024]{1,0:T(4,128)S(1)}, f32[4,1024]{1,0:T(4,128)S(1)}, f32[16,8,4,1024]{3,2,1,0:T(4,128)S(1)}...) while((s32[]{:T(128)}, f32[4,1024]{1,0:T(4,128)S(1)}, ...), condition=%wide.region_6.6_spmd.clone, body=%wide.region_5.5_spmd.clone.sunk | while | flops 832281 | bytes 1364985 | solution.py:110
  204.6 2.5 fusion.179
  251.3 2.5 fusion.179
  263.0 2.5 fusion.179
  274.7 2.5 fusion.179
  286.4 2.5 fusion.179
  333.2 2.5 fusion.179
  344.9 2.5 fusion.179
  356.6 2.5 fusion.179
  387.8 187.1 %while.60 = (s32[]{:T(128)}, f32[4,1024]{1,0:T(4,128)S(1)}, f32[4,1024]{1,0:T(4,128)S(1)}, f32[4,1024]{1,0:T(4,128)S(1)}, f32[16,8,4,1024]{3,2,1,0:T(4,128)S(1)}...) while((s32[]{:T(128)}, f32[4,1024]{1,0:T(4,128)S(1)}, ...), condition=%wide.region_6.6_spmd.clone, body=%wide.region_5.5_spmd.clone.sunk | while | flops 832281 | bytes 1364985 | solution.py:110
  419.3 2.5 fusion.179
  431.0 2.5 fusion.179
  442.7 2.5 fusion.179
  454.4 2.5 fusion.179
  501.2 2.5 fusion.179
  512.9 2.5 fusion.179
  524.6 2.5 fusion.179
  571.4 2.5 fusion.179
  579.2 187.1 %while.60 = (s32[]{:T(128)}, f32[4,1024]{1,0:T(4,128)S(1)}, f32[4,1024]{1,0:T(4,128)S(1)}, f32[4,1024]{1,0:T(4,128)S(1)}, f32[16,8,4,1024]{3,2,1,0:T(4,128)S(1)}...) while((s32[]{:T(128)}, f32[4,1024]{1,0:T(4,128)S(1)}, ...), condition=%wide.region_6.6_spmd.clone, body=%wide.region_5.5_spmd.clone.sunk | while | flops 832281 | bytes 1364985 | solution.py:110
  610.7 2.5 fusion.179
  622.4 2.5 fusion.179
  634.1 2.5 fusion.179
  645.8 2.5 fusion.179
  692.6 2.5 fusion.179
  704.3 2.5 fusion.179
  716.0 2.5 fusion.179
  762.8 2.5 fusion.179
  770.6 187.1 %while.60 = (s32[]{:T(128)}, f32[4,1024]{1,0:T(4,128)S(1)}, f32[4,1024]{1,0:T(4,128)S(1)}, f32[4,1024]{1,0:T(4,128)S(1)}, f32[16,8,4,1024]{3,2,1,0:T(4,128)S(1)}...) while((s32[]{:T(128)}, f32[4,1024]{1,0:T(4,128)S(1)}, ...), condition=%wide.region_6.6_spmd.clone, body=%wide.region_5.5_spmd.clone.sunk | while | flops 832281 | bytes 1364985 | solution.py:110
  813.8 2.5 fusion.179
  825.5 2.5 fusion.179
  837.2 2.5 fusion.179
  884.0 2.5 fusion.179
  895.7 2.5 fusion.179
  907.4 2.5 fusion.179
  919.1 2.5 fusion.179
  960.7 5.0 copy.35
  965.8 10.7 reshape.753
  976.5 14.9 %all-to-all-start = ((f32[64,1,1536]{2,1,0:T(1,128)}), f32[64,1,1536]{2,1,0:T(1,128)S(1)}, u32[]{:S(2)}, u32[]{:S(2)}) async-start(f32[64,1,1536]{2,1,0:T(1,128)} %reshape.753), calls=%async_computation | async-start | bytes 786432 | tf_op jit(solution)/shard_map/all_to_all | solution.py:198
  991.8 3.2 fusion.103
  995.0 12.2 %all-to-all-done = f32[64,1,1536]{2,1,0:T(1,128)S(1)} async-done(((f32[64,1,1536]{2,1,0:T(1,128)}), f32[64,1,1536]{2,1,0:T(1,128)S(1)}, u32[]{:S(2)}, u32[]{:S(2)}) %all-to-all-start) | async-done | bytes 393248 | tf_op jit(solution)/shard_map/all_to_all | solution.py:198
  1009.3 11.3 %reshape.754 = f32[1024,6,2,8]{3,2,1,0:T(2,128)} reshape(f32[64,1536]{1,0:T(8,128)S(1)} %reduce.2) | data formatting | bytes 786432
  1020.6 7.3 copy.46
  1030.8 3.2 collective-permute-start
  1034.1 2.6 collective-permute-start.1
  1036.8 7.0 collective-permute-done.1
  1048.3 5.3 collective-permute-done.3
  1055.7 8.1 collective-permute-start.5
  1069.7 5.3 collective-permute-done.7
  1075.4 8.4 collective-permute-start.8
  1085.7 7.8 collective-permute-done.9
  1098.0 5.3 collective-permute-done.11
  1105.4 8.1 collective-permute-start.13
  1119.4 5.3 collective-permute-done.15
  (1850 shorter events, 483.9 us)
Async XLA Ops:
  965.8 25.6 %copy-start.1 = (s32[256]{0:T(256)S(1)}, s32[256]{0:T(256)}, u32[]{:S(2)}) copy-start(s32[256]{0:T(256)} %param.7) | copy-start | bytes 3076
  976.5 30.7 %all-to-all-start = ((f32[64,1,1536]{2,1,0:T(1,128)}), f32[64,1,1536]{2,1,0:T(1,128)S(1)}, u32[]{:S(2)}, u32[]{:S(2)}) async-start(f32[64,1,1536]{2,1,0:T(1,128)} %reshape.753), calls=%async_computation | async-start | bytes 786432 | tf_op jit(solution)/shard_map/all_to_all | solution.py:198
  1030.8 5.9 collective-permute-start
  1034.1 9.7 collective-permute-start.1
  1043.9 4.4 collective-permute-start.2
  1045.8 7.8 collective-permute-start.3
  1053.8 10.1 collective-permute-start.4
  1055.7 9.5 collective-permute-start.5
  1065.3 4.4 collective-permute-start.6
  1067.2 7.8 collective-permute-start.7
  1075.4 10.3 collective-permute-start.8
  1083.8 9.7 collective-permute-start.9
  1093.6 4.4 collective-permute-start.10
  1095.6 7.8 collective-permute-start.11
  1103.5 22.2 %copy-start = (f32[3,2,16,256]{3,2,1,0:T(8,128)}, f32[3,2,16,256]{3,2,1,0:T(8,128)S(1)}, u32[]{:S(2)}) copy-start(f32[3,2,16,256]{3,2,1,0:T(8,128)S(1)} %get-tuple-element.812) | copy-start | bytes 294916
  1103.5 10.1 collective-permute-start.12
  1105.4 9.5 collective-permute-start.13
  1115.0 4.4 collective-permute-start.14
  1117.0 7.8 collective-permute-start.15
where the time goes:
time: 1140 us; the launch traced here: 1130 us
  other arithmetic  486 us (43%)
  loops' own time  409 us (36%)
  local copies, waits for them, and re-layouts  96.7 us (8%)
  starting transfers between devices  68.5 us (6%)
  waiting for transfers between devices  50.8 us (4%)
  matrix products  13.7 us (1%)
    another operation x5, loops' own time, run_block(): rec_state, values = lax.scan(advance, rec_state, step_values, unroll=8)  403 us
    sqrt x240, other arithmetic, advance(): jnp.sqrt(jnp.maximum(4.0 * degree * degree - 1.0, 1.0) / jnp.maximum(degr...  204 us
    eq x400, other arithmetic, advance(): starting = (degree == order_now)[:, None]  197 us
    while x560, other arithmetic  57.7 us
    slice x80, local copies, waits for them, and re-layouts, run_block(): rec_state, values = lax.scan(advance, rec_state, step_values, unroll=8)  48.3 us
    ppermute x8, waiting for transfers between devices, with_halo(): before = lax.ppermute(last, axis, up)  36 us
    ppermute x8, starting transfers between devices, with_halo(): after = lax.ppermute(first, axis, down)  35.6 us
    unnamed x8, local copies, waits for them, and re-layouts  23 us
  transfers between devices with their start and end apart: 17, of which 9 were waited for; matrix products, arithmetic and copies ran while one was open for 0% of the time, Pallas kernels for 0%

commit v1 on v0

--- a/solution.py
+++ b/solution.py
@@ -195,7 +195,13 @@
     angles = row_angles(jnp.arange(row_total, dtype=jnp.int32), row_total)
     spectral = synthesize(coefficients, own_pairs, angles, order_total)
     synth_grid = transform(
-        lax.all_to_all(spectral, "lat", split_axis=3, concat_axis=0, tiled=True), own_table
+        jnp.concatenate(
+            lax.all_to_all(
+                jnp.stack(jnp.split(spectral, lax.axis_size("lat"), axis=3)), "lat", 0, 0
+            ),
+            axis=0,
+        ),
+        own_table,
     )
     potential = synth_grid.reshape(3, levels, band_rows, sector_cols)
     global_rows = lat_pos * band_rows + jnp.arange(-2, band_rows + 2, dtype=jnp.int32)

time: 1140 us -> 1100 us (0.965)
  the two profiles are of different devices: /device:TPU:8 before, /device:TPU:40 now
where the time goes in v1:
time: 1100 us; the launch traced here: 1090 us
  other arithmetic  481 us (44%)
  loops' own time  405 us (37%)
  local copies, waits for them, and re-layouts  74 us (7%)
  starting transfers between devices  68.5 us (6%)
  waiting for transfers between devices  50.8 us (5%)
  matrix products  12.5 us (1%)
    another operation x5, loops' own time, run_block(): rec_state, values = lax.scan(advance, rec_state, step_values, unroll=8)  398 us
    sqrt x240, other arithmetic, advance(): jnp.sqrt(jnp.maximum(4.0 * degree * degree - 1.0, 1.0) / jnp.maximum(degr...  204 us
    eq x400, other arithmetic, advance(): starting = (degree == order_now)[:, None]  193 us
    while x560, other arithmetic  57.7 us
    slice x80, local copies, waits for them, and re-layouts, run_block(): rec_state, values = lax.scan(advance, rec_state, step_values, unroll=8)  48.4 us
    ppermute x8, waiting for transfers between devices, with_halo(): before = lax.ppermute(last, axis, up)  36 us
    ppermute x8, starting transfers between devices, with_halo(): after = lax.ppermute(first, axis, down)  35.6 us
  transfers between devices with their start and end apart: 17, of which 9 were waited for; matrix products, arithmetic and copies ran while one was open for 0% of the time, Pallas kernels for 0%

profile of v1, /device:TPU:40, one launch (start us, length us, event | category | flops | bytes accessed | tf_op | source)
XLA Modules:
  0.0 1092.6 jit_solution(4528682196705908075)
XLA Ops:
  3.7 948.0 %while.59 = (s32[]{:T(128)}, f32[4,1024]{1,0:T(4,128)S(1)}, f32[4,1024]{1,0:T(4,128)S(1)}, f32[4,1024]{1,0:T(4,128)S(1)}, f32[4,2,12,1024]{3,2,1,0:T(8,128)S(1)}...) while((s32[]{:T(128)}, f32[4,1024]{1,0:T(4,128)S(1)}, ...), condition=%wide.region_7.8_spmd.clone.clone.clone.clone, body=%wide.region_4.7_spmd.clone.clone.clone.clone.sunk | while | flops 152044704 | bytes 4487110 | solution.py:123
  5.1 185.2 %while.60 = (s32[]{:T(128)}, f32[4,1024]{1,0:T(4,128)S(1)}, f32[4,1024]{1,0:T(4,128)S(1)}, f32[4,1024]{1,0:T(4,128)S(1)}, f32[16,8,4,1024]{3,2,1,0:T(4,128)S(1)}...) while((s32[]{:T(128)}, f32[4,1024]{1,0:T(4,128)S(1)}, ...), condition=%wide.region_6.6_spmd.clone, body=%wide.region_5.5_spmd.clone.sunk | while | flops 832281 | bytes 1364985 | solution.py:110
  13.1 2.5 fusion.180
  24.7 2.5 fusion.180
  36.3 2.5 fusion.180
  47.9 2.5 fusion.180
  59.4 2.5 fusion.180
  71.0 2.5 fusion.180
  82.6 2.5 fusion.180
  94.1 2.5 fusion.180
  105.7 2.5 fusion.180
  117.3 2.5 fusion.180
  128.9 2.5 fusion.180
  140.4 2.5 fusion.180
  194.7 185.2 %while.60 = (s32[]{:T(128)}, f32[4,1024]{1,0:T(4,128)S(1)}, f32[4,1024]{1,0:T(4,128)S(1)}, f32[4,1024]{1,0:T(4,128)S(1)}, f32[16,8,4,1024]{3,2,1,0:T(4,128)S(1)}...) while((s32[]{:T(128)}, f32[4,1024]{1,0:T(4,128)S(1)}, ...), condition=%wide.region_6.6_spmd.clone, body=%wide.region_5.5_spmd.clone.sunk | while | flops 832281 | bytes 1364985 | solution.py:110
  202.7 2.5 fusion.180
  295.3 2.5 fusion.180
  306.9 2.5 fusion.180
  318.5 2.5 fusion.180
  330.0 2.5 fusion.180
  341.6 2.5 fusion.180
  353.2 2.5 fusion.180
  364.7 2.5 fusion.180
  376.3 2.5 fusion.180
  384.3 185.2 %while.60 = (s32[]{:T(128)}, f32[4,1024]{1,0:T(4,128)S(1)}, f32[4,1024]{1,0:T(4,128)S(1)}, f32[4,1024]{1,0:T(4,128)S(1)}, f32[16,8,4,1024]{3,2,1,0:T(4,128)S(1)}...) while((s32[]{:T(128)}, f32[4,1024]{1,0:T(4,128)S(1)}, ...), condition=%wide.region_6.6_spmd.clone, body=%wide.region_5.5_spmd.clone.sunk | while | flops 832281 | bytes 1364985 | solution.py:110
  473.3 2.5 fusion.180
  484.9 2.5 fusion.180
  496.5 2.5 fusion.180
  508.1 2.5 fusion.180
  519.6 2.5 fusion.180
  531.2 2.5 fusion.180
  542.8 2.5 fusion.180
  554.3 2.5 fusion.180
  565.9 2.5 fusion.180
  573.9 185.2 %while.60 = (s32[]{:T(128)}, f32[4,1024]{1,0:T(4,128)S(1)}, f32[4,1024]{1,0:T(4,128)S(1)}, f32[4,1024]{1,0:T(4,128)S(1)}, f32[16,8,4,1024]{3,2,1,0:T(4,128)S(1)}...) while((s32[]{:T(128)}, f32[4,1024]{1,0:T(4,128)S(1)}, ...), condition=%wide.region_6.6_spmd.clone, body=%wide.region_5.5_spmd.clone.sunk | while | flops 832281 | bytes 1364985 | solution.py:110
  581.9 2.5 fusion.180
  674.5 2.5 fusion.180
  686.1 2.5 fusion.180
  697.7 2.5 fusion.180
  709.2 2.5 fusion.180
  720.8 2.5 fusion.180
  732.4 2.5 fusion.180
  743.9 2.5 fusion.180
  755.5 2.5 fusion.180
  763.5 185.2 %while.60 = (s32[]{:T(128)}, f32[4,1024]{1,0:T(4,128)S(1)}, f32[4,1024]{1,0:T(4,128)S(1)}, f32[4,1024]{1,0:T(4,128)S(1)}, f32[16,8,4,1024]{3,2,1,0:T(4,128)S(1)}...) while((s32[]{:T(128)}, f32[4,1024]{1,0:T(4,128)S(1)}, ...), condition=%wide.region_6.6_spmd.clone, body=%wide.region_5.5_spmd.clone.sunk | while | flops 832281 | bytes 1364985 | solution.py:110
  771.5 2.5 fusion.180
  783.1 2.5 fusion.180
  875.7 2.5 fusion.180
  887.3 2.5 fusion.180
  898.8 2.5 fusion.180
  958.9 14.9 %all-to-all-start = ((f32[64,1,1536]{2,1,0:T(1,128)}), f32[64,1,1536]{2,1,0:T(1,128)S(1)}, u32[]{:S(2)}, u32[]{:S(2)}) async-start(f32[64,1,1536]{2,1,0:T(1,128)} %reshape.756), calls=%async_computation | async-start | bytes 786432 | tf_op jit(solution)/shard_map/all_to_all | solution.py:199
  974.1 3.3 fusion.103
  977.4 12.2 %all-to-all-done = f32[64,1,1536]{2,1,0:T(1,128)S(1)} async-done(((f32[64,1,1536]{2,1,0:T(1,128)}), f32[64,1,1536]{2,1,0:T(1,128)S(1)}, u32[]{:S(2)}, u32[]{:S(2)}) %all-to-all-start) | async-done | bytes 393248 | tf_op jit(solution)/shard_map/all_to_all | solution.py:199
  997.7 3.2 collective-permute-start
  1000.9 2.6 collective-permute-start.1
  1003.6 7.0 collective-permute-done.1
  1015.2 5.3 collective-permute-done.3
  1022.6 8.1 collective-permute-start.5
  1036.6 5.3 collective-permute-done.7
  1042.2 8.4 collective-permute-start.8
  1052.6 7.8 collective-permute-done.9
  1064.9 5.3 collective-permute-done.11
  1072.3 8.1 collective-permute-start.13
  1086.3 5.3 collective-permute-done.15
  (1918 shorter events, 479.5 us)
Async XLA Ops:
  955.5 18.3 %copy-start.3 = (s32[256]{0:T(256)S(1)}, s32[256]{0:T(256)}, u32[]{:S(2)}) copy-start(s32[256]{0:T(256)} %param.7) | copy-start | bytes 3076
  958.9 30.7 %all-to-all-start = ((f32[64,1,1536]{2,1,0:T(1,128)}), f32[64,1,1536]{2,1,0:T(1,128)S(1)}, u32[]{:S(2)}, u32[]{:S(2)}) async-start(f32[64,1,1536]{2,1,0:T(1,128)} %reshape.756), calls=%async_computation | async-start | bytes 786432 | tf_op jit(solution)/shard_map/all_to_all | solution.py:199
  994.6 2.4 copy-start
  994.6 2.4 copy-start.1
  997.7 5.9 collective-permute-start
  1000.9 9.7 collective-permute-start.1
  1010.8 4.4 collective-permute-start.2
  1012.7 7.8 collective-permute-start.3
  1020.7 10.1 collective-permute-start.4
  1022.6 9.5 collective-permute-start.5
  1032.2 4.4 collective-permute-start.6
  1034.1 7.8 collective-permute-start.7
  1042.2 10.3 collective-permute-start.8
  1050.6 9.7 collective-permute-start.9
  1060.5 4.4 collective-permute-start.10
  1062.4 7.8 collective-permute-start.11
  1070.4 22.2 %copy-start.2 = (f32[3,2,16,256]{3,2,1,0:T(8,128)}, f32[3,2,16,256]{3,2,1,0:T(8,128)S(1)}, u32[]{:S(2)}) copy-start(f32[3,2,16,256]{3,2,1,0:T(8,128)S(1)} %get-tuple-element.812) | copy-start | bytes 294916
  1070.4 10.1 collective-permute-start.12
  1072.3 9.5 collective-permute-start.13
  1081.9 4.4 collective-permute-start.14
  1083.8 7.8 collective-permute-start.15
